TPU v7x, 32 devices: a whole 2x2x4 slice. The times are simulated.
32 devices in a mesh: chan: 8 (over y, x, core), rec: 4 (over z).
Axes of the slice: x: 2, y: 2, z: 4, core: 2. Of those that a mesh axis runs over, the one named last changes fastest.
Arguments:
- records: bfloat16 [4, 4096, 2048], P('rec', 'chan'), as said below
- fir_choice: int32 [2048], P('chan'), may hold values from 0 to 15
- bank: float32 [16, 64], replicated, may hold values from -4 to 4
- partner: int32 [3, 8], replicated, may hold values from 0 to 7, as said below
Outputs:
- xcorr: float32 [3, 2048, 8, 256], P(None, 'chan', 'rec')
Inputs may be any that keep to these rules, and one draw needn't show every extreme that they name: Each round is a pairing by exclusive or: partner[r, a] = a XOR m_r for one mask m_r of 1 to 7 a round, the masks of different rounds differ. `records`: samples are finite and not all zero in any channel of any record.
All inputs are finite; a program needn't handle non-finite values.
Results may differ from a plain program's by a relative error of at most 0.0055.
Values may be sent and summed in bfloat16 or wider, within the bound.
No kernel may reach another device: no remote copies, remote signals or barrier semaphores. Data moves between devices by JAX's collectives and lax.ppermute only.
A program may use at most 128 MiB of HBM per device.

v0:
```python
import math

import jax
import jax.numpy as jnp
from jax import lax
from jax.sharding import PartitionSpec as P

LAGS = 8
ROUNDS = 3


def partner_2(x, axis, apart):
    return lax.ppermute(x, axis, [(i, i ^ 1 << apart) for i in range(lax.axis_size(axis))])


def whiten_block(raw, taps):
    length = raw.shape[0]
    width = taps.shape[1]
    signal = raw.astype(jnp.float32)
    padded = jnp.pad(signal, ((width - 1, 0), (0, 0)))
    total = jnp.zeros(signal.shape, jnp.float32)
    for tap in range(width):
        total = (
            total + taps[:, tap][None, :] * padded[width - 1 - tap : width - 1 - tap + length, :]
        )
    whitened = total.astype(jnp.bfloat16)
    values = whitened.astype(jnp.float32)
    power = jnp.mean(values * values, axis=0)
    return (values * lax.rsqrt(power + 1e-06)[None, :]).astype(jnp.bfloat16)


def lagged_term(own, mate):
    length = own.shape[0]
    padded = jnp.pad(mate, ((0, LAGS), (0, 0)))
    stacked = jnp.concatenate([padded[lag : lag + length, :] for lag in range(LAGS)], axis=1)
    product = lax.dot_general(
        own, stacked, (((0,), (0,)), ((), ())), preferred_element_type=jnp.float32
    )
    return (product * (1.0 / math.sqrt(length))).reshape(own.shape[1], LAGS, own.shape[1])


def per_device(records, fir_choice, bank, partner):
    blocks_all = lax.axis_size("chan")
    width = records.shape[2] // blocks_all
    span = records.shape[1]
    local = records[0].reshape(span, blocks_all, width)
    owned = lax.all_to_all(local, "chan", split_axis=1, concat_axis=0, tiled=True)[:, 0, :]
    onehot = (fir_choice[:, None] == jnp.arange(bank.shape[0], dtype=jnp.int32)[None, :]).astype(
        jnp.float32
    )
    taps = jnp.dot(
        onehot, bank, precision=lax.Precision.HIGHEST, preferred_element_type=jnp.float32
    )
    normed = whiten_block(owned, taps)
    terms = []
    levels = blocks_all.bit_length() - 1
    for step in range(ROUNDS):
        mask = partner[step, 0]
        moving = normed
        for level in range(levels):
            flag = jnp.bitwise_and(jnp.right_shift(mask, level), 1) == 1
            swapped = partner_2(moving, "chan", level)
            moving = jnp.where(flag, swapped, moving)
        terms.append(lagged_term(normed, moving))
    summed = [lax.psum_scatter(term, "rec", scatter_dimension=1, tiled=True) for term in terms]
    return jnp.stack(summed, axis=0)


def solution(mesh):
    placed = (P("rec", "chan", None), P("chan"), P(), P())
    return jax.shard_map(
        per_device,
        mesh=mesh,
        in_specs=placed,
        out_specs=P(None, "chan", "rec", None),
        check_vma=False,
    )
```

profile of v0, /device:TPU:0, one launch (start us, length us, event | category | flops | bytes accessed | tf_op | source)
XLA Modules:
  0.0 489.9 jit_solution(24298019512525007)
XLA Ops:
  6.5 4.0 copy.7
  10.5 5.2 %all-to-all-start = ((bf16[512,8,256]{0,2,1:T(8,128)(2,1)}), bf16[512,8,256]{0,2,1:T(8,128)(2,1)}, u32[]{:S(2)}, u32[]{:S(2)}) async-start(bf16[512,8,256]{0,2,1:T(8,128)(2,1)} %bitcast.107), calls=%async_computation | async-start | bytes 4194304 | tf_op jit(solution)/shard_map/all_to_all | solution.py:47
  16.2 26.3 %all-to-all-done = bf16[512,8,256]{0,2,1:T(8,128)(2,1)} async-done(((bf16[512,8,256]{0,2,1:T(8,128)(2,1)}), bf16[512,8,256]{0,2,1:T(8,128)(2,1)}, u32[]{:S(2)}, u32[]{:S(2)}) %all-to-all-start) | async-done | bytes 2097184 | tf_op jit(solution)/shard_map/all_to_all | solution.py:47
  42.4 4.1 convert_bitcast_fusion
  46.5 5.4 %copy.8 = f32[8,512,1,256]{3,1,0,2:T(8,128)} copy(f32[8,512,1,256]{1,3,0,2:T(8,128)} %convert_bitcast_fusion) | data formatting | bytes 8388608 | tf_op jit(solution)/shard_map/convert_element_type | solution.py:19
  52.0 135.3 %fusion = (f32[256]{0:T(256)S(1)}, bf16[4096,256]{1,0:T(8,128)(2,1)}) fusion(f32[256]{0:T(256)S(1)} %bitcast.121, f32[256]{0:T(256)S(1)} %bitcast.122, f32[256]{0:T(256)S(1)} %bitcast.123, f32[256]{0:T(256)S(1)} %bitcast.124, f32[256]{0:T(256)S(1)} %bitcast.125, f32[256]{0:T(256)S(1)} %bitcast.126, f32[256]{0:T(256)S(1)} %bitcast.127, f32[256]{0:T(256)S(1)} %bitcast.128, ...), kind=kLoop, calls=%fused_computation.2 | loop fusion | flops 137363200 | bytes 6358016 | tf_op jit(solution)/shard_map/reduce_sum | solution.py:28
  187.3 2.2 fusion.1
  189.6 0.6 fusion.8
  192.1 1.7 collective-permute-done
  194.3 0.6 collective-permute-start.1
  194.8 1.5 collective-permute-start.3
  200.1 0.6 collective-permute-start.5
  200.7 42.1 %collective-permute-done.1 = bf16[4096,256]{1,0:T(8,128)(2,1)S(1)} collective-permute-done((bf16[4096,256]{1,0:T(8,128)(2,1)S(1)}, bf16[4096,256]{1,0:T(8,128)(2,1)S(1)}, u32[]{:S(2)}, u32[]{:S(2)}) %collective-permute-start.1) | collective-permute-done | bytes 2097184 | tf_op jit(solution)/shard_map/ppermute | solution.py:13
  243.1 0.6 collective-permute-start.2
  243.7 44.0 %collective-permute-done.3 = bf16[4096,256]{1,0:T(8,128)(2,1)S(1)} collective-permute-done((bf16[4096,256]{1,0:T(8,128)(2,1)S(1)}, bf16[4096,256]{1,0:T(8,128)(2,1)S(1)}, u32[]{:S(2)}, u32[]{:S(2)}) %collective-permute-start.3) | collective-permute-done | bytes 2097184 | tf_op jit(solution)/shard_map/ppermute | solution.py:13
  287.8 1.6 broadcast_select_fusion.4
  289.9 42.0 %collective-permute-done.5 = bf16[4096,256]{1,0:T(8,128)(2,1)S(1)} collective-permute-done((bf16[4096,256]{1,0:T(8,128)(2,1)S(1)}, bf16[4096,256]{1,0:T(8,128)(2,1)S(1)}, u32[]{:S(2)}, u32[]{:S(2)}) %collective-permute-start.5) | collective-permute-done | bytes 2097184 | tf_op jit(solution)/shard_map/ppermute | solution.py:13
  331.9 1.6 broadcast_select_fusion.1
  334.0 0.6 constant_dynamic-update-slice_fusion
  338.5 4.5 convolution_multiply_fusion.2
  343.0 1.5 copy.21
  344.8 2.2 constant_dynamic-update-slice_fusion.1
  350.8 4.5 convolution_multiply_fusion.1
  355.4 1.5 copy.20
  357.3 23.4 %collective-permute-done.6 = bf16[4096,256]{1,0:T(8,128)(2,1)} collective-permute-done((bf16[4096,256]{1,0:T(8,128)(2,1)}, bf16[4096,256]{1,0:T(8,128)(2,1)}, u32[]{:S(2)}, u32[]{:S(2)}) %collective-permute-start.6) | collective-permute-done | bytes 2097184 | tf_op jit(solution)/shard_map/ppermute | solution.py:13
  380.7 2.2 constant_dynamic-update-slice_fusion.2
  386.7 4.5 convolution_multiply_fusion
  391.3 1.5 copy.19
  392.8 41.5 %reduce-scatter.6.cloned.1.call-done = f32[256,2,256]{2,0,1:T(8,128)} async-done(((f32[256,8,256]{2,0,1:T(8,128)}), f32[256,2,256]{2,0,1:T(8,128)}) %reduce-scatter.6.cloned.1.call-update) | async-done | bytes 524304 | tf_op jit(solution)/shard_map/reduce_scatter | solution.py:65
  434.3 45.2 %reduce-scatter.8.cloned.1.call-done = f32[256,2,256]{2,0,1:T(8,128)} async-done(((f32[256,8,256]{2,0,1:T(8,128)}), f32[256,2,256]{2,0,1:T(8,128)}) %reduce-scatter.8.cloned.1.call-update) | async-done | bytes 524304 | tf_op jit(solution)/shard_map/reduce_scatter | solution.py:65
  479.5 1.5 pad_maximum_fusion
  481.0 2.4 copy.12
  (51 shorter events, 14.2 us)
Async XLA Ops:
  6.5 9.2 %copy-start = (f32[16,64]{1,0:T(8,128)S(1)}, f32[16,64]{1,0:T(8,128)}, u32[]{:S(2)}) copy-start(f32[16,64]{1,0:T(8,128)} %param.6) | copy-start | bytes 12292
  6.5 9.2 %copy-start.4 = (s32[256]{0:T(256)S(1)}, s32[256]{0:T(256)}, u32[]{:S(2)}) copy-start(s32[256]{0:T(256)} %param.5) | copy-start | bytes 3076
  10.5 31.9 %all-to-all-start = ((bf16[512,8,256]{0,2,1:T(8,128)(2,1)}), bf16[512,8,256]{0,2,1:T(8,128)(2,1)}, u32[]{:S(2)}, u32[]{:S(2)}) async-start(bf16[512,8,256]{0,2,1:T(8,128)(2,1)} %bitcast.107), calls=%async_computation | async-start | bytes 4194304 | tf_op jit(solution)/shard_map/all_to_all | solution.py:47
  15.7 377.1 %reduce-scatter.4.cloned.1.call-start = ((), (), s32[]{:S(2)}) async-start(), calls=%async_computation.4 | async-start | bytes 2621440 | tf_op jit(solution)/shard_map/reduce_scatter | solution.py:65
  52.0 137.6 %copy-start.3 = (s32[3,8]{1,0:T(4,128)S(1)}, s32[3,8]{1,0:T(4,128)}, u32[]{:S(2)}) copy-start(s32[3,8]{1,0:T(4,128)} %param.7) | copy-start | bytes 292
  187.3 6.4 %copy-start.2 = (bf16[4096,256]{1,0:T(8,128)(2,1)S(1)}, bf16[4096,256]{1,0:T(8,128)(2,1)}, u32[]{:S(2)}) copy-start(bf16[4096,256]{1,0:T(8,128)(2,1)} %get-tuple-element.12) | copy-start | bytes 6291460
  189.5 4.2 collective-permute-start
  194.3 48.6 %collective-permute-start.1 = (bf16[4096,256]{1,0:T(8,128)(2,1)S(1)}, bf16[4096,256]{1,0:T(8,128)(2,1)S(1)}, u32[]{:S(2)}, u32[]{:S(2)}) collective-permute-start(bf16[4096,256]{1,0:T(8,128)(2,1)S(1)} %get-tuple-element.13), channel_id=1, source_target_pairs={{0,8},{4,12},{8,0},{12,4},{16,24},{20,28},{24,16},{28,20},{1,9},{5... | collective-permute-start | bytes 6291464 | tf_op jit(solution)/shard_map/ppermute | solution.py:13
  194.8 92.9 %collective-permute-start.3 = (bf16[4096,256]{1,0:T(8,128)(2,1)S(1)}, bf16[4096,256]{1,0:T(8,128)(2,1)S(1)}, u32[]{:S(2)}, u32[]{:S(2)}) collective-permute-start(bf16[4096,256]{1,0:T(8,128)(2,1)S(1)} %get-tuple-element.15), channel_id=1, source_target_pairs={{0,8},{4,12},{8,0},{12,4},{16,24},{20,28},{24,16},{28,20},{1,9},{5... | collective-permute-start | bytes 6291464 | tf_op jit(solution)/shard_map/ppermute | solution.py:13
  200.1 131.7 %collective-permute-start.5 = (bf16[4096,256]{1,0:T(8,128)(2,1)S(1)}, bf16[4096,256]{1,0:T(8,128)(2,1)S(1)}, u32[]{:S(2)}, u32[]{:S(2)}) collective-permute-start(bf16[4096,256]{1,0:T(8,128)(2,1)S(1)} %get-tuple-element.14), channel_id=1, source_target_pairs={{0,8},{4,12},{8,0},{12,4},{16,24},{20,28},{24,16},{28,20},{1,9},{5... | collective-permute-start | bytes 6291464 | tf_op jit(solution)/shard_map/ppermute | solution.py:13
  243.1 90.9 %collective-permute-start.2 = (bf16[4096,256]{1,0:T(8,128)(2,1)S(1)}, bf16[4096,256]{1,0:T(8,128)(2,1)S(1)}, u32[]{:S(2)}, u32[]{:S(2)}) collective-permute-start(bf16[4096,256]{1,0:T(8,128)(2,1)S(1)} %broadcast_select_fusion.7), channel_id=1, source_target_pairs={{0,16},{4,20},{8,24},{12,28},{16,0},{20,4},{24,8},{28,12},{1,17},{... | collective-permute-start | bytes 6291464 | tf_op jit(solution)/shard_map/ppermute | solution.py:13
  289.4 55.4 %collective-permute-start.4 = (bf16[4096,256]{1,0:T(8,128)(2,1)}, bf16[4096,256]{1,0:T(8,128)(2,1)}, u32[]{:S(2)}, u32[]{:S(2)}) collective-permute-start(bf16[4096,256]{1,0:T(8,128)(2,1)} %broadcast_select_fusion.4), channel_id=1, source_target_pairs={{0,16},{4,20},{8,24},{12,28},{16,0},{20,4},{24,8},{28,12},{1,17},{... | collective-permute-start | bytes 6291464 | tf_op jit(solution)/shard_map/ppermute | solution.py:13
  333.5 47.2 %collective-permute-start.6 = (bf16[4096,256]{1,0:T(8,128)(2,1)}, bf16[4096,256]{1,0:T(8,128)(2,1)}, u32[]{:S(2)}, u32[]{:S(2)}) collective-permute-start(bf16[4096,256]{1,0:T(8,128)(2,1)} %broadcast_select_fusion.1), channel_id=1, source_target_pairs={{0,16},{4,20},{8,24},{12,28},{16,0},{20,4},{24,8},{28,12},{1,17},{... | collective-permute-start | bytes 6291464 | tf_op jit(solution)/shard_map/ppermute | solution.py:13
  344.5 89.8 %reduce-scatter.6.cloned.1.call-start = ((), (), s32[]{:S(2)}) async-start(), calls=%async_computation.5 | async-start | bytes 2621440 | tf_op jit(solution)/shard_map/reduce_scatter | solution.py:65
  356.9 122.5 %reduce-scatter.8.cloned.1.call-start = ((), (), s32[]{:S(2)}) async-start(), calls=%async_computation.6 | async-start | bytes 2621440 | tf_op jit(solution)/shard_map/reduce_scatter | solution.py:65
  392.7 90.6 %copy-start.1 = (f32[16,64]{1,0:T(8,128)S(1)}, f32[16,64]{1,0:T(8,128)}, u32[]{:S(2)}) copy-start(f32[16,64]{1,0:T(8,128)} %param.6) | copy-start | bytes 12292
Sparse Core Ops, SparseCore 0:
  344.7 44.4 reduce-scatter.3
  391.4 42.8 reduce-scatter.5
  436.6 42.8 reduce-scatter.7
where the time goes:
time: 490 us
  waiting for transfers between devices  266 us (54%)
  other arithmetic  152 us (31%)
  local copies, waits for them, and re-layouts  28.1 us (6%)
  between operations  19.1 us (4%)
  matrix products  13.9 us (3%)
  starting transfers between devices  10.3 us (2%)
    ppermute x7, waiting for transfers between devices, partner_2(): lax.ppermute(x, axis, [(i, i ^ 1 << apart) for i in range(lax.axis_size(a...  153 us
    reduce_sum x1, other arithmetic, whiten_block(): power = jnp.mean(values * values, axis=0)  135 us
    reduce_scatter x3, waiting for transfers between devices, per_device(): lax.psum_scatter(term, 'rec', scatter_dimension=1, tiled=True)  86.7 us
    all_to_all x1, waiting for transfers between devices, per_device(): lax.all_to_all(local, 'chan', split_axis=1, concat_axis=0, tiled=True)  26.3 us
    dot_general x3, matrix products, lagged_term(): lax.dot_general(own, stacked, (((0,), (0,)), ((), ())), preferred_element...  13.6 us
    unnamed x29, local copies, waits for them, and re-layouts  13.6 us
  transfers between devices with their start and end apart: 11, of which 8 were waited for; matrix products, arithmetic and copies ran while one was open for 8% of the time, Pallas kernels for 0%

commit v1 on v0

--- a/solution.py
+++ b/solution.py
@@ -1,12 +1,374 @@
+import functools
 import math
 
 import jax
 import jax.numpy as jnp
 from jax import lax
+from jax.experimental import pallas as pl
+from jax.experimental.pallas import tpu as pltpu
 from jax.sharding import PartitionSpec as P
+
 
 LAGS = 8
 ROUNDS = 3
+EXT = 8
+HALO = 80
+LANES = 128
+F32 = jnp.float32
+BF16 = jnp.bfloat16
+
+
+def swap(x, axis, mask):
+    return lax.ppermute(x, axis, [(i, i ^ mask) for i in range(lax.axis_size(axis))])
+
+
+def whiten_kernel(start, me_ref, x_ref, halo_ref, c0, c1, c2, c3, bank_ref, w_ref, p_ref, xe, tp, ws):
+    taps = bank_ref.shape[1]
+    span = x_ref.shape[0]
+    xe[0:HALO, :] = halo_ref[...].astype(F32)
+    xe[HALO : HALO + span, :] = x_ref[...].astype(F32)
+    mask = jnp.bitwise_xor(pl.program_id(0) + start, me_ref[0])
+    row, which = jnp.bitwise_and(mask, 1), jnp.right_shift(mask, 1)
+    choice = c0[row]
+    for index, other in ((1, c1), (2, c2), (3, c3)):
+        choice = jnp.where(which == index, other[row], choice)
+    for group in range(taps // 8):
+        table = jnp.zeros((8, LANES), F32)
+        for entry in range(bank_ref.shape[0]):
+            table = jnp.where(choice == entry, bank_ref[entry, 8 * group : 8 * group + 8, :], table)
+        for sub in range(8):
+            tp[8 * group + sub] = jnp.broadcast_to(table[sub : sub + 1, :], (8, LANES))
+    tiles = (EXT + span) // 8
+    per = 13
+    first = HALO - EXT
+
+    def group_body(g, carry):
+        base = pl.multiple_of(g * (per * 8), 8)
+        acc = [jnp.zeros((8, LANES), F32) for _ in range(per)]
+        for sub in range(8):
+            coef = [tp[8 * q + sub] for q in range(taps // 8)]
+            for v in range(1 - taps // 8, per):
+                tile = xe[pl.ds(base + (first + 8 * v - sub), 8), :]
+                for q in range(taps // 8):
+                    if 0 <= v + q < per:
+                        acc[v + q] = acc[v + q] + coef[q] * tile
+        for i in range(per):
+            ws[pl.ds(base + 8 * i, 8), :] = acc[i]
+        return carry
+
+    lax.fori_loop(0, tiles // per, group_body, 0)
+    rounded = ws[...].astype(BF16)
+    w_ref[...] = rounded
+    own = rounded.astype(F32)[EXT:, :]
+    p_ref[0] = jnp.sum(own * own, axis=0, keepdims=True)
+
+
+def whiten(me, x, halo, choices, bank, half, quad):
+    span = x.shape[0]
+    blocks = len(choices)
+    start = quad * blocks
+    lane = lambda b, m: (0, 2 * (b + start) + half)
+    return pl.pallas_call(
+        functools.partial(whiten_kernel, start),
+        out_shape=(
+            jax.ShapeDtypeStruct((EXT + span, blocks * LANES), BF16),
+            jax.ShapeDtypeStruct((blocks, 1, LANES), F32),
+        ),
+        grid_spec=pltpu.PrefetchScalarGridSpec(
+            num_scalar_prefetch=1,
+            grid=(blocks,),
+            in_specs=[
+                pl.BlockSpec((span, LANES), lane),
+                pl.BlockSpec((HALO, LANES), lane),
+                *[pl.BlockSpec((2, 1, LANES), lambda b, m: (0, 0, half))] * blocks,
+                pl.BlockSpec(bank.shape, lambda b, m: (0, 0, 0)),
+            ],
+            out_specs=[
+                pl.BlockSpec((EXT + span, LANES), lambda b, m: (0, b)),
+                pl.BlockSpec((1, 1, LANES), lambda b, m: (b, 0, 0)),
+            ],
+            scratch_shapes=[
+                pltpu.VMEM((HALO + span, LANES), F32),
+                pltpu.VMEM((bank.shape[1], 8, LANES), F32),
+                pltpu.VMEM((EXT + span, LANES), F32),
+            ],
+        ),
+        compiler_params=pltpu.CompilerParams(vmem_limit_bytes=12 * 2**20),
+        cost_estimate=pl.CostEstimate(flops=5 * 10**9, bytes_accessed=2**20, transcendentals=0),
+    )(me, x, halo, *choices, bank)
+
+
+def correlate_kernel(spans, halves, carried, last, *refs):
+    ids = refs[0]
+    scales = refs[1 : 1 + halves]
+    at = 1 + halves
+    pieces = refs[at : at + 2 * halves * spans]
+    at += 2 * halves * spans
+    jobs = 1 if halves == 1 else 2
+    acc_in = refs[at : at + jobs] if carried else None
+    at += jobs if carried else 0
+    chunks = 1 if halves == 1 else 3
+    outs = refs[at : at + ((3 if chunks == 1 else 10) if last else jobs)]
+    at += len(outs)
+    a_buf, b_buf, a_norm, shift0, shift1, turn0, turn1, sem = refs[at : at + 8]
+    accs = refs[at + 8 : at + 8 + jobs] if last else outs
+    a_shift, b_turn = (shift0, shift1), (turn0, turn1)
+    length = b_buf.shape[3]
+    third = ROUNDS * LANES
+    roles = 1 + ROUNDS
+    pairs = spans // 2
+
+    def copy(k, h, role, quad):
+        column = pl.ds(pl.multiple_of(ids[roles + role] * LANES, LANES), LANES)
+        source = pieces[(k * halves + h) * 2 + quad]
+        if role == 0:
+            return pltpu.make_async_copy(source.at[:, column], a_buf.at[k, h], sem.at[k, h, role])
+        return pltpu.make_async_copy(
+            source.at[pl.ds(EXT, length), column], b_buf.at[k, h, role - 1], sem.at[k, h, role]
+        )
+
+    for k in range(spans):
+        for h in range(halves):
+            for role in range(roles):
+                upper = ids[role] >= 4
+
+                @pl.when(upper)
+                def _(k=k, h=h, role=role):
+                    copy(k, h, role, 1).start()
+
+                @pl.when(jnp.logical_not(upper))
+                def _(k=k, h=h, role=role):
+                    copy(k, h, role, 0).start()
+
+    own_scale = [scales[h][ids[0]] for h in range(halves)]
+    mate_scale = [[scales[h][ids[1 + r]] for r in range(ROUNDS)] for h in range(halves)]
+    place = [
+        pl.multiple_of(ids[2 * roles + lag] * LANES, LANES) for lag in range(LAGS)
+    ]
+
+    def arrive(pair):
+        for k in (2 * pair, 2 * pair + 1):
+            for h in range(halves):
+                for role in range(roles):
+                    copy(k, h, role, 0).wait()
+
+    def prepare(pair):
+        steps = []
+        for j in range(2):
+            k = 2 * pair + j
+            rows = slice(j * length, (j + 1) * length)
+            for h in range(halves):
+
+                def normalize(k=k, j=j, h=h):
+                    a_norm[j, h] = a_buf[k, h].astype(F32) * own_scale[h]
+
+                steps.append(normalize)
+                for lag in range(LAGS):
+
+                    def shift(j=j, h=h, rows=rows, lag=lag):
+                        moved = a_norm[j, h, EXT - lag : EXT - lag + length, :]
+                        a_shift[pair % 2][h, rows, pl.ds(place[lag], LANES)] = moved.astype(BF16)
+
+                    steps.append(shift)
+                for r in range(ROUNDS):
+
+                    def turn(k=k, h=h, rows=rows, r=r):
+                        scaled = (b_buf[k, h, r].astype(F32) * mate_scale[h][r]).astype(BF16)
+                        top = h * third + r * LANES
+                        b_turn[pair % 2][top : top + LANES, rows] = scaled.T
+
+                    steps.append(turn)
+        return steps
+
+    def contract(pair, job, c):
+        low = third if halves == 2 and job == 0 else 0
+        column = slice(c * 2 * LANES, (c + 1) * 2 * LANES)
+        product = jnp.dot(
+            b_turn[pair % 2][low:, :],
+            a_shift[pair % 2][job, :, column],
+            preferred_element_type=F32,
+        )
+        if pair > 0:
+            product = product + accs[job][:, column]
+        elif carried:
+            product = product + acc_in[job][:, column]
+        if pair < pairs - 1 or not last:
+            accs[job][:, column] = product
+            return
+        product = product * (1.0 / math.sqrt(8 * length))
+        for part in range(product.shape[0] // third):
+            value = product[part * third : (part + 1) * third, :]
+            chunk = job + part
+            if chunk == 2:
+                outs[6 + c][...] = value.astype(outs[6 + c].dtype)
+            elif c < 2:
+                outs[3 * chunk][:, column] = value.astype(BF16)
+            else:
+                outs[3 * chunk + c - 1][...] = value
+
+    arrive(0)
+    for step in prepare(0):
+        step()
+    for pair in range(pairs):
+        steps = []
+        if pair + 1 < pairs:
+            arrive(pair + 1)
+            steps = prepare(pair + 1)
+        turns = [(job, c) for job in range(jobs) for c in range(LAGS // 2)]
+        each = -(-len(steps) // len(turns))
+        for at_turn, (job, c) in enumerate(turns):
+            contract(pair, job, c)
+            for step in steps[at_turn * each : (at_turn + 1) * each]:
+                step()
+
+
+def correlate(ids, scales, pieces, carried, last):
+    spans, halves = len(pieces), len(pieces[0])
+    rows = pieces[0][0][0].shape[0]
+    length = rows - EXT
+    third = ROUNDS * LANES
+    wide = LAGS * LANES
+    sizes = [third] if halves == 1 else [third, 2 * third]
+    chunks = 1 if halves == 1 else 3
+    vmem = pl.BlockSpec(memory_space=pltpu.VMEM)
+    anywhere = pl.BlockSpec(memory_space=pl.ANY)
+    if last:
+        shapes = [
+            jax.ShapeDtypeStruct((third, 4 * LANES), BF16),
+            jax.ShapeDtypeStruct((third, 2 * LANES), F32),
+            jax.ShapeDtypeStruct((third, 2 * LANES), F32),
+        ] * min(chunks, 2)
+        if chunks == 3:
+            shapes += [jax.ShapeDtypeStruct((third, 2 * LANES), BF16)] * 3
+            shapes += [jax.ShapeDtypeStruct((third, 2 * LANES), F32)]
+    else:
+        shapes = [jax.ShapeDtypeStruct((size, wide), F32) for size in sizes]
+    flat = [pieces[k][h][q] for k in range(spans) for h in range(halves) for q in range(2)]
+    flops = 2 * spans * length * sum(sizes) * wide
+    return pl.pallas_call(
+        functools.partial(correlate_kernel, spans, halves, carried is not None, last),
+        out_shape=shapes,
+        in_specs=[pl.BlockSpec(memory_space=pltpu.SMEM)]
+        + [vmem] * halves
+        + [anywhere] * len(flat)
+        + [vmem] * len(carried or []),
+        out_specs=[vmem] * len(shapes),
+        scratch_shapes=[
+            pltpu.VMEM((spans, halves, rows, LANES), BF16),
+            pltpu.VMEM((spans, halves, ROUNDS, length, LANES), BF16),
+            pltpu.VMEM((2, halves, rows, LANES), F32),
+            pltpu.VMEM((halves, 2 * length, wide), BF16),
+            pltpu.VMEM((halves, 2 * length, wide) if spans > 2 else (8, LANES), BF16),
+            pltpu.VMEM((halves * third, 2 * length), BF16),
+            pltpu.VMEM((halves * third, 2 * length) if spans > 2 else (8, LANES), BF16),
+            pltpu.SemaphoreType.DMA((spans, halves, 1 + ROUNDS)),
+        ]
+        + ([pltpu.VMEM((size, wide), F32) for size in sizes] if last else []),
+        compiler_params=pltpu.CompilerParams(vmem_limit_bytes=30 * 2**20),
+        cost_estimate=pl.CostEstimate(
+            flops=2 * flops, bytes_accessed=spans * 2**19, transcendentals=0
+        ),
+    )(ids, *scales, *flat, *(carried or []))
+
+
+def finish_kernel(*refs):
+    out = refs[-1]
+    at = 0
+    for chunk in range(4):
+        hi, hj = chunk >> 1, chunk & 1
+        count = 4 if chunk == 3 else 3
+        total = refs[at][...]
+        for other in refs[at + 1 : at + count]:
+            total = total + other[:, other.shape[1] - 2 * LANES :].astype(F32)
+        at += count
+        for r in range(ROUNDS):
+            for p in range(out.shape[2]):
+                tile = total[r * LANES : (r + 1) * LANES, p * LANES : (p + 1) * LANES]
+                out[r, hi * LANES : (hi + 1) * LANES, p, hj * LANES : (hj + 1) * LANES] = tile.T
+
+
+def finish(parts):
+    flat = [value for part in parts for value in part]
+    return pl.pallas_call(
+        finish_kernel,
+        out_shape=jax.ShapeDtypeStruct((ROUNDS, 2 * LANES, 2, 2 * LANES), F32),
+        in_specs=[pl.BlockSpec(memory_space=pltpu.VMEM)] * len(flat),
+        out_specs=pl.BlockSpec(memory_space=pltpu.VMEM),
+        compiler_params=pltpu.CompilerParams(vmem_limit_bytes=12 * 2**20),
+        cost_estimate=pl.CostEstimate(flops=10**6, bytes_accessed=4 * 2**20, transcendentals=0),
+        name="finish",
+    )(*flat)
+
+
+def per_device_cube(records, fir_choice, bank, partner):
+    return cube_body(records, fir_choice, bank, partner)
+
+
+def cube_body(records, fir_choice, bank, partner):
+    x = records[0]
+    span = x.shape[0]
+    blocks = lax.axis_size("chan")
+    me = lax.axis_index("chan").astype(jnp.int32)
+    z = lax.axis_index("rec")
+    choice = fir_choice[None, None, :]
+    wide = jnp.broadcast_to(bank[:, :, None], bank.shape + (LANES,))
+    beside = swap(choice, "chan", 1)
+    beside, wide = lax.optimization_barrier((beside, wide))
+    choice = jnp.concatenate([choice, beside], axis=0)
+    halo = lax.ppermute(x[span - HALO :, :], "chan", [(i, i + 1) for i in range(blocks - 1)])
+    choices = [choice] + [swap(choice, "chan", m) for m in (2, 4, 6)]
+
+    zl, zh = jnp.bitwise_and(z, 1), jnp.right_shift(z, 1)
+    places = []
+    for lag in range(LAGS):
+        keep = (((lag >> 1) & 1) == zl).astype(jnp.int32)
+        mine = ((lag >> 2) == zh).astype(jnp.int32)
+        places.append(keep * 4 + mine * 2 + (lag & 1))
+    mates = lax.dynamic_index_in_dim(partner, me, axis=1, keepdims=False)
+    roles = jnp.concatenate([me[None], mates])
+    ids = jnp.concatenate([roles, jnp.bitwise_and(roles, 3), jnp.stack(places)])
+
+    own, beside_x, beside_y, across = {}, {}, {}, {}
+    scales = []
+    for h in range(2):
+        power = []
+        for q in range(2):
+            own[h, q], squares = whiten(me[None], x, halo, choices, wide, h, q)
+            power.append(squares)
+            beside_x[h, q] = swap(own[h, q], "chan", 2)
+            beside_y[h, q] = swap(own[h, q], "chan", 4)
+        total = jnp.concatenate(power, axis=0)
+        total = total + swap(total, "chan", 1)
+        others = [swap(total, "chan", m) for m in (2, 4, 6)]
+        total = total + others[0] + (others[1] + others[2])
+        scales.append(lax.rsqrt(total * (1.0 / (blocks * span)) + 1e-06))
+        across[h, 0] = swap(beside_y[h, 0], "chan", 2)
+        across[h, 1] = swap(beside_x[h, 1], "chan", 4)
+
+    def both(piece, h):
+        mine = [piece[h, q] for q in range(2)]
+        return mine, [swap(mine[q], "chan", 1) for q in range(2)]
+
+    groups = [own, beside_x, beside_y, across]
+    spans = []
+    for h in range(2):
+        spans.append([s for piece in groups for s in both(piece, h)])
+
+    def exchange(send, far, near):
+        first = swap(send, "rec", 1)
+        handed = (far + first[:, : 2 * LANES].astype(F32)).astype(BF16)
+        return near, first, swap(handed, "rec", 2)
+
+    early = correlate(ids, scales[:1], [[s] for s in spans[0]], None, True)
+    parts = [exchange(*early)]
+    late = [[spans[0][k], spans[1][k]] for k in range(8)]
+    held = correlate(ids, scales, late[:6], None, False)
+    rest = correlate(ids, scales, late[6:], held, True)
+    direct = [swap(rest[6 + c], "rec", m) for c, m in ((1, 1), (0, 3), (2, 2))]
+    parts.append(exchange(*rest[0:3]))
+    parts.append(exchange(*rest[3:6]))
+    parts.append((rest[9], *direct))
+    return finish(parts)
 
 
 def partner_2(x, axis, apart):
@@ -68,8 +430,9 @@
 
 def solution(mesh):
     placed = (P("rec", "chan", None), P("chan"), P(), P())
+    cube = mesh.shape["chan"] == 8 and mesh.shape["rec"] == 4
     return jax.shard_map(
-        per_device,
+        per_device_cube if cube else per_device,
         mesh=mesh,
         in_specs=placed,
         out_specs=P(None, "chan", "rec", None),

time: 490 us -> 228 us (0.47)
  waiting for transfers between devices: 266 us -> 96.5 us
  other arithmetic: 152 us -> 0.96 us
  Pallas kernels: 0 us -> 61.2 us
  starting transfers between devices: 10.3 us -> 51 us
  between operations: 19.1 us -> 0.3 us
  matrix products: 13.9 us -> 0 us
  local copies, waits for them, and re-layouts: 28.1 us -> 17.8 us
    reduce_sum x1 -> x0, other arithmetic: 135 us -> none  [whiten_block(): power = jnp.mean(values * values, axis=0)]
    reduce_scatter x3 -> x0, waiting for transfers between devices: 86.7 us -> none  [per_device(): lax.psum_scatter(term, 'rec', scatter_dimension=1, tiled=True)]
    pallas_call x0 -> x8, Pallas kernels: none -> 61.2 us  [the longest x4 31.3 us: whiten(): pl.pallas_call(functools.partial(whiten_kernel, start), out_shape=(jax.Sh...]
    ppermute x7 -> x50, waiting for transfers between devices: 153 us -> 96.5 us  [the longest x49 96.5 us: swap(): lax.ppermute(x, axis, [(i, i ^ mask) for i in range(lax.axis_size(axis))])]
    ppermute x7 -> x50, starting transfers between devices: 4.48 us -> 51 us  [the longest x49 48.6 us: swap(): lax.ppermute(x, axis, [(i, i ^ mask) for i in range(lax.axis_size(axis))])]
    all_to_all x1 -> x0, waiting for transfers between devices: 26.3 us -> none  [per_device(): lax.all_to_all(local, 'chan', split_axis=1, concat_axis=0, tiled=True)]
    dot_general x4 -> x0, matrix products: 13.9 us -> none  [the longest x3 13.6 us: lagged_term(): lax.dot_general(own, stacked, (((0,), (0,)), ((), ())), preferred_element...]
    convert_element_type x2 -> x3, other arithmetic: 6.26 us -> 0.15 us  [exchange(): handed = (far + first[:, :2 * LANES].astype(F32)).astype(BF16)]
  transfers between devices with their start and end apart: 11 -> 50, of which waited for: 8 -> 24; matrix products, arithmetic and copies ran while one was open for 8% -> 1% of each run, Pallas kernels for 0% -> 20%
where the time goes in v1:
time: 228 us
  waiting for transfers between devices  96.5 us (42%)
  Pallas kernels  61.2 us (27%)
  starting transfers between devices  51 us (22%)
  local copies, waits for them, and re-layouts  17.8 us (8%)
    ppermute x49, waiting for transfers between devices, swap(): lax.ppermute(x, axis, [(i, i ^ mask) for i in range(lax.axis_size(axis))])  96.5 us
    ppermute x49, starting transfers between devices, swap(): lax.ppermute(x, axis, [(i, i ^ mask) for i in range(lax.axis_size(axis))])  48.6 us
    pallas_call x4, Pallas kernels, whiten(): pl.pallas_call(functools.partial(whiten_kernel, start), out_shape=(jax.Sh...  31.3 us
    pallas_call x3, Pallas kernels, correlate(): pl.pallas_call(functools.partial(correlate_kernel, spans, halves, carried...  27.7 us
    unnamed x46, local copies, waits for them, and re-layouts  15.7 us
  transfers between devices with their start and end apart: 50, of which 24 were waited for; matrix products, arithmetic and copies ran while one was open for 1% of the time, Pallas kernels for 20%

profile of v1, /device:TPU:0, one launch (start us, length us, event | category | flops | bytes accessed | tf_op | source)
XLA Modules:
  0.0 227.8 jit_solution(5835656559106157591)
XLA Ops:
  1.0 2.4 %collective-permute-start = (bf16[80,2048]{1,0:T(8,128)(2,1)S(1)}, bf16[80,2048]{1,0:T(8,128)(2,1)S(1)}, u32[]{:S(2)}, u32[]{:S(2)}) collective-permute-start(bf16[80,2048]{1,0:T(8,128)(2,1)S(1)} %slice_bitcast_fusion), channel_id=1, source_target_pairs={{0,4},{4,8},{8,12},{12,16},{16,20},{20,24},{24,28},{1,5},{5,9},{9,... | collective-permute-start | bytes 983048 | tf_op jit(solution)/shard_map/ppermute | solution.py:318
  3.4 2.6 %collective-permute-start.1 = (s32[1,1,256]{2,1,0:T(1,128)}, s32[1,1,256]{2,1,0:T(1,128)S(1)}, u32[]{:S(2)}, u32[]{:S(2)}) collective-permute-start(s32[1,1,256]{2,1,0:T(1,128)} %bitcast.17), channel_id=1, source_target_pairs={{0,4},{4,0},{8,12},{12,8},{16,20},{20,16},{24,28},{28,24},{1,5},{5... | collective-permute-start | bytes 3080 | tf_op jit(solution)/shard_map/ppermute | solution.py:22
  16.5 7.8 %shard_map.47 = (bf16[520,512]{1,0:T(8,128)(2,1)S(1)}, f32[4,1,128]{2,1,0:T(1,128)S(1)}) custom-call(s32[1]{0:T(128)} %bitcast.me_ref, bf16[512,2048]{1,0:T(8,128)(2,1)S(1)} %bitcast.13, bf16[80,2048]{1,0:T(8,128)(2,1)S(1)} %collective-permute-done.halo_ref, s32[2,1,256]{2,1,0:T(1,128)S(1)} %pad_add_fusion.c0, s32[2,1,256]{2,1,0:T(1,128)S(1)} %collective-permute-done.2.c1, ...), custom_call_target="tpu_custom_call" | custom-call | flops 5000000000 | bytes 1048576 | tf_op jit(solution)/shard_map/pallas_call | solution.py:71
  24.4 1.9 collective-permute-start.12
  26.7 7.8 %shard_map.46 = (bf16[520,512]{1,0:T(8,128)(2,1)S(1)}, f32[4,1,128]{2,1,0:T(1,128)S(1)}) custom-call(s32[1]{0:T(128)} %bitcast.me_ref, bf16[512,2048]{1,0:T(8,128)(2,1)S(1)} %bitcast.14, bf16[80,2048]{1,0:T(8,128)(2,1)S(1)} %collective-permute-done.halo_ref, s32[2,1,256]{2,1,0:T(1,128)S(1)} %pad_add_fusion.c0, s32[2,1,256]{2,1,0:T(1,128)S(1)} %collective-permute-done.2.c1, ...), custom_call_target="tpu_custom_call" | custom-call | flops 5000000000 | bytes 1048576 | tf_op jit(solution)/shard_map/pallas_call | solution.py:71
  36.4 7.8 %shard_map.49 = (bf16[520,512]{1,0:T(8,128)(2,1)S(1)}, f32[4,1,128]{2,1,0:T(1,128)S(1)}) custom-call(s32[1]{0:T(128)} %bitcast.me_ref, bf16[512,2048]{1,0:T(8,128)(2,1)S(1)} %bitcast.15, bf16[80,2048]{1,0:T(8,128)(2,1)S(1)} %collective-permute-done.halo_ref, s32[2,1,256]{2,1,0:T(1,128)S(1)} %pad_add_fusion.c0, s32[2,1,256]{2,1,0:T(1,128)S(1)} %collective-permute-done.2.c1, ...), custom_call_target="tpu_custom_call" | custom-call | flops 5000000000 | bytes 1048576 | tf_op jit(solution)/shard_map/pallas_call | solution.py:71
  44.2 7.9 %shard_map.50 = (bf16[520,512]{1,0:T(8,128)(2,1)S(1)}, f32[4,1,128]{2,1,0:T(1,128)S(1)}) custom-call(s32[1]{0:T(128)} %bitcast.me_ref, bf16[512,2048]{1,0:T(8,128)(2,1)S(1)} %bitcast.16, bf16[80,2048]{1,0:T(8,128)(2,1)S(1)} %collective-permute-done.halo_ref, s32[2,1,256]{2,1,0:T(1,128)S(1)} %pad_add_fusion.c0, s32[2,1,256]{2,1,0:T(1,128)S(1)} %collective-permute-done.2.c1, ...), custom_call_target="tpu_custom_call" | custom-call | flops 5000000000 | bytes 1048576 | tf_op jit(solution)/shard_map/pallas_call | solution.py:71
  54.5 1.8 collective-permute-start.26
  56.3 1.8 collective-permute-done.26
  59.9 1.9 collective-permute-done.27
  63.5 2.8 %collective-permute-done.28 = f32[8,1,128]{2,1,0:T(1,128)S(1)} collective-permute-done((f32[8,1,128]{2,1,0:T(1,128)S(1)}, f32[8,1,128]{2,1,0:T(1,128)S(1)}, u32[]{:S(2)}, u32[]{:S(2)}) %collective-permute-start.28) | collective-permute-done | bytes 4128 | tf_op jit(solution)/shard_map/ppermute | solution.py:22
  68.0 1.8 collective-permute-done.6
  71.6 1.9 collective-permute-done.7
  75.2 2.8 %collective-permute-done.8 = f32[8,1,128]{2,1,0:T(1,128)S(1)} collective-permute-done((f32[8,1,128]{2,1,0:T(1,128)S(1)}, f32[8,1,128]{2,1,0:T(1,128)S(1)}, u32[]{:S(2)}, u32[]{:S(2)}) %collective-permute-start.8) | collective-permute-done | bytes 4128 | tf_op jit(solution)/shard_map/ppermute | solution.py:22
  82.3 8.9 %collective-permute-done.31.refs_14_ = bf16[520,512]{1,0:T(8,128)(2,1)} collective-permute-done((bf16[520,512]{1,0:T(8,128)(2,1)S(1)}, bf16[520,512]{1,0:T(8,128)(2,1)}, u32[]{:S(2)}, u32[]{:S(2)}) %collective-permute-start.31) | collective-permute-done | bytes 532512 | tf_op jit(solution)/shard_map/ppermute | solution.py:22
  91.2 2.0 collective-permute-start.40
  96.5 2.3 collective-permute-done.37.refs_13_
  104.9 2.0 collective-permute-start.20
  109.4 10.7 %collective-permute-done.20.refs_15_.refs_4_ = bf16[520,512]{1,0:T(8,128)(2,1)} collective-permute-done((bf16[520,512]{1,0:T(8,128)(2,1)S(1)}, bf16[520,512]{1,0:T(8,128)(2,1)}, u32[]{:S(2)}, u32[]{:S(2)}) %collective-permute-start.20) | collective-permute-done | bytes 532512 | tf_op jit(solution)/shard_map/ppermute | solution.py:22
  120.1 1.9 collective-permute-done.19.refs_14_.refs_3_
  122.0 10.7 %collective-permute-done.30.refs_5_ = bf16[520,512]{1,0:T(8,128)(2,1)} collective-permute-done((bf16[520,512]{1,0:T(8,128)(2,1)}, bf16[520,512]{1,0:T(8,128)(2,1)}, u32[]{:S(2)}, u32[]{:S(2)}) %collective-permute-start.30) | collective-permute-done | bytes 532512 | tf_op jit(solution)/shard_map/ppermute | solution.py:22
  141.6 13.8 %shard_map.51 = (f32[384,1024]{1,0:T(8,128)S(1)}, f32[768,1024]{1,0:T(8,128)S(1)}) custom-call(s32[16]{0:T(128)S(1)} %concatenate.17.refs_0_, f32[8,1,128]{2,1,0:T(1,128)S(1)} %add_rsqrt_fusion.1.refs_1_, f32[8,1,128]{2,1,0:T(1,128)S(1)} %add_rsqrt_fusion.refs_2_, bf16[520,512]{1,0:T(8,128)(2,1)S(1)} %get-tuple-element.34.refs_2_.refs_3_, ...), custom_call_target="tpu_custom_call" | custom-call | flops 14495514624 | bytes 3145728 | tf_op jit(solution)/shard_map/pallas_call | solution.py:248
  155.4 5.9 %shard_map.52 = (bf16[384,512]{1,0:T(8,128)(2,1)S(1)}, f32[384,256]{1,0:T(8,128)S(1)}, f32[384,256]{1,0:T(8,128)S(1)}, bf16[384,512]{1,0:T(8,128)(2,1)S(1)}, f32...) custom-call(s32[16]{0:T(128)S(1)} %concatenate.17.refs_0_, ...), custom_call_target="tpu_custom_call" | custom-call | flops 4831838208 | bytes 1048576 | tf_op jit(solution)/shard_map/pallas_call | solution.py:248
  165.1 2.5 %collective-permute-start.48 = (bf16[384,256]{1,0:T(8,128)(2,1)S(1)}, bf16[384,256]{1,0:T(8,128)(2,1)S(1)}, u32[]{:S(2)}, u32[]{:S(2)}) collective-permute-start(bf16[384,256]{1,0:T(8,128)(2,1)S(1)} %get-tuple-element.53), channel_id=1, source_target_pairs={{0,3},{1,2},{2,1},{3,0},{4,7},{5,6},{6,5},{7,4},{8,11},{9,10},{10,... | collective-permute-start | bytes 589832 | tf_op jit(solution)/shard_map/ppermute | solution.py:22
  167.7 8.0 %shard_map.48 = (bf16[384,512]{1,0:T(8,128)(2,1)S(1)}, f32[384,256]{1,0:T(8,128)S(1)}, f32[384,256]{1,0:T(8,128)S(1)}) custom-call(s32[16]{0:T(128)S(1)} %concatenate.17.refs_0_, f32[8,1,128]{2,1,0:T(1,128)S(1)} %add_rsqrt_fusion.1.refs_1_, bf16[520,512]{1,0:T(8,128)(2,1)S(1)} %get-tuple-element.34.refs_2_.refs_3_, ...), custom_call_target="tpu_custom_call" | custom-call | flops 6442450944 | bytes 4194304 | tf_op jit(solution)/shard_map/pallas_call | solution.py:248
  175.7 2.0 collective-permute-done.45.refs_7_
  177.7 8.4 %collective-permute-done.43.refs_4_ = bf16[384,512]{1,0:T(8,128)(2,1)S(1)} collective-permute-done((bf16[384,512]{1,0:T(8,128)(2,1)S(1)}, bf16[384,512]{1,0:T(8,128)(2,1)S(1)}, u32[]{:S(2)}, u32[]{:S(2)}) %collective-permute-start.43) | collective-permute-done | bytes 393248 | tf_op jit(solution)/shard_map/ppermute | solution.py:22
  186.1 5.7 %collective-permute-start.46 = (bf16[384,256]{1,0:T(8,128)(2,1)S(1)}, bf16[384,256]{1,0:T(8,128)(2,1)S(1)}, u32[]{:S(2)}, u32[]{:S(2)}) collective-permute-start(bf16[384,256]{1,0:T(8,128)(2,1)S(1)} %add_convert_fusion), channel_id=1, source_target_pairs={{0,2},{1,3},{2,0},{3,1},{4,6},{5,7},{6,4},{7,5},{8,10},{9,11},{10,... | collective-permute-start | bytes 589832 | tf_op jit(solution)/shard_map/ppermute | solution.py:22
  191.9 14.3 %collective-permute-done.23.refs_1_ = bf16[384,512]{1,0:T(8,128)(2,1)S(1)} collective-permute-done((bf16[384,512]{1,0:T(8,128)(2,1)S(1)}, bf16[384,512]{1,0:T(8,128)(2,1)S(1)}, u32[]{:S(2)}, u32[]{:S(2)}) %collective-permute-start.23) | collective-permute-done | bytes 393248 | tf_op jit(solution)/shard_map/ppermute | solution.py:22
  209.2 13.3 %collective-permute-done.44.refs_5_ = bf16[384,256]{1,0:T(8,128)(2,1)S(1)} collective-permute-done((bf16[384,256]{1,0:T(8,128)(2,1)S(1)}, bf16[384,256]{1,0:T(8,128)(2,1)S(1)}, u32[]{:S(2)}, u32[]{:S(2)}) %collective-permute-start.44) | collective-permute-done | bytes 196640 | tf_op jit(solution)/shard_map/ppermute | solution.py:22
  222.6 3.1 %collective-permute-done.24.refs_2_ = bf16[384,256]{1,0:T(8,128)(2,1)S(1)} collective-permute-done((bf16[384,256]{1,0:T(8,128)(2,1)S(1)}, bf16[384,256]{1,0:T(8,128)(2,1)S(1)}, u32[]{:S(2)}, u32[]{:S(2)}) %collective-permute-start.24) | collective-permute-done | bytes 196640 | tf_op jit(solution)/shard_map/ppermute | solution.py:22
  225.7 2.2 finish.1
  (137 shorter events, 57.0 us)
Async XLA Ops:
  1.0 13.9 %collective-permute-start = (bf16[80,2048]{1,0:T(8,128)(2,1)S(1)}, bf16[80,2048]{1,0:T(8,128)(2,1)S(1)}, u32[]{:S(2)}, u32[]{:S(2)}) collective-permute-start(bf16[80,2048]{1,0:T(8,128)(2,1)S(1)} %slice_bitcast_fusion), channel_id=1, source_target_pairs={{0,4},{4,8},{8,12},{12,16},{16,20},{20,24},{24,28},{1,5},{5,9},{9,... | collective-permute-start | bytes 983048 | tf_op jit(solution)/shard_map/ppermute | solution.py:318
  24.4 55.4 %collective-permute-start.12 = (bf16[520,512]{1,0:T(8,128)(2,1)S(1)}, bf16[520,512]{1,0:T(8,128)(2,1)S(1)}, u32[]{:S(2)}, u32[]{:S(2)}) collective-permute-start(bf16[520,512]{1,0:T(8,128)(2,1)S(1)} %get-tuple-element.35.refs_3_.refs_4_), channel_id=1, source_target_pairs={{0,8},{4,12},{8,0},{12,4},{16,24},{20,28},{24,16},{28,20},{1,9},{5... | collective-permute-start | bytes 1597448 | tf_op jit(solution)/shard_map/ppermute | solution.py:22
  26.2 54.1 %collective-permute-start.16 = (bf16[520,512]{1,0:T(8,128)(2,1)S(1)}, bf16[520,512]{1,0:T(8,128)(2,1)S(1)}, u32[]{:S(2)}, u32[]{:S(2)}) collective-permute-start(bf16[520,512]{1,0:T(8,128)(2,1)S(1)} %get-tuple-element.35.refs_3_.refs_4_), channel_id=1, source_target_pairs={{0,16},{4,20},{8,24},{12,28},{16,0},{20,4},{24,8},{28,12},{1,17},{... | collective-permute-start | bytes 1597448 | tf_op jit(solution)/shard_map/ppermute | solution.py:22
  34.6 45.7 %collective-permute-start.15 = (bf16[520,512]{1,0:T(8,128)(2,1)S(1)}, bf16[520,512]{1,0:T(8,128)(2,1)S(1)}, u32[]{:S(2)}, u32[]{:S(2)}) collective-permute-start(bf16[520,512]{1,0:T(8,128)(2,1)S(1)} %get-tuple-element.34.refs_2_.refs_3_), channel_id=1, source_target_pairs={{0,16},{4,20},{8,24},{12,28},{16,0},{20,4},{24,8},{28,12},{1,17},{... | collective-permute-start | bytes 1597448 | tf_op jit(solution)/shard_map/ppermute | solution.py:22
  36.1 44.7 %collective-permute-start.11 = (bf16[520,512]{1,0:T(8,128)(2,1)S(1)}, bf16[520,512]{1,0:T(8,128)(2,1)}, u32[]{:S(2)}, u32[]{:S(2)}) collective-permute-start(bf16[520,512]{1,0:T(8,128)(2,1)S(1)} %get-tuple-element.34.refs_2_.refs_3_), channel_id=1, source_target_pairs={{0,8},{4,12},{8,0},{12,4},{16,24},{20,28},{24,16},{28,20},{1,9},{5... | collective-permute-start | bytes 1597448 | tf_op jit(solution)/shard_map/ppermute | solution.py:22
  78.0 13.2 %collective-permute-start.31 = (bf16[520,512]{1,0:T(8,128)(2,1)S(1)}, bf16[520,512]{1,0:T(8,128)(2,1)}, u32[]{:S(2)}, u32[]{:S(2)}) collective-permute-start(bf16[520,512]{1,0:T(8,128)(2,1)S(1)} %get-tuple-element.42.refs_6_), channel_id=1, source_target_pairs={{0,8},{4,12},{8,0},{12,4},{16,24},{20,28},{24,16},{28,20},{1,9},{5... | collective-permute-start | bytes 1597448 | tf_op jit(solution)/shard_map/ppermute | solution.py:22
  79.8 13.7 %collective-permute-start.29 = (bf16[520,512]{1,0:T(8,128)(2,1)S(1)}, bf16[520,512]{1,0:T(8,128)(2,1)}, u32[]{:S(2)}, u32[]{:S(2)}) collective-permute-start(bf16[520,512]{1,0:T(8,128)(2,1)S(1)} %get-tuple-element.41.refs_5_), channel_id=1, source_target_pairs={{0,16},{4,20},{8,24},{12,28},{16,0},{20,4},{24,8},{28,12},{1,17},{... | collective-permute-start | bytes 1597448 | tf_op jit(solution)/shard_map/ppermute | solution.py:22
  80.3 13.2 %collective-permute-start.10 = (bf16[520,512]{1,0:T(8,128)(2,1)S(1)}, bf16[520,512]{1,0:T(8,128)(2,1)S(1)}, u32[]{:S(2)}, u32[]{:S(2)}) collective-permute-start(bf16[520,512]{1,0:T(8,128)(2,1)S(1)} %get-tuple-element.35.refs_3_.refs_4_), channel_id=1, source_target_pairs={{0,4},{4,0},{8,12},{12,8},{16,20},{20,16},{24,28},{28,24},{1,5},{5... | collective-permute-start | bytes 1597448 | tf_op jit(solution)/shard_map/ppermute | solution.py:22
  80.3 15.4 %collective-permute-start.9 = (bf16[520,512]{1,0:T(8,128)(2,1)S(1)}, bf16[520,512]{1,0:T(8,128)(2,1)S(1)}, u32[]{:S(2)}, u32[]{:S(2)}) collective-permute-start(bf16[520,512]{1,0:T(8,128)(2,1)S(1)} %get-tuple-element.34.refs_2_.refs_3_), channel_id=1, source_target_pairs={{0,4},{4,0},{8,12},{12,8},{16,20},{20,16},{24,28},{28,24},{1,5},{5... | collective-permute-start | bytes 1597448 | tf_op jit(solution)/shard_map/ppermute | solution.py:22
  80.8 18.0 %collective-permute-start.37 = (bf16[520,512]{1,0:T(8,128)(2,1)S(1)}, bf16[520,512]{1,0:T(8,128)(2,1)}, u32[]{:S(2)}, u32[]{:S(2)}) collective-permute-start(bf16[520,512]{1,0:T(8,128)(2,1)S(1)} %get-tuple-element.41.refs_5_), channel_id=1, source_target_pairs={{0,8},{4,12},{8,0},{12,4},{16,24},{20,28},{24,16},{28,20},{1,9},{5... | collective-permute-start | bytes 1597448 | tf_op jit(solution)/shard_map/ppermute | solution.py:22
  91.2 9.3 %collective-permute-start.40 = (bf16[520,512]{1,0:T(8,128)(2,1)S(1)}, bf16[520,512]{1,0:T(8,128)(2,1)S(1)}, u32[]{:S(2)}, u32[]{:S(2)}) collective-permute-start(bf16[520,512]{1,0:T(8,128)(2,1)S(1)} %get-tuple-element.42.refs_6_), channel_id=1, source_target_pairs={{0,16},{4,20},{8,24},{12,28},{16,0},{20,4},{24,8},{28,12},{1,17},{... | collective-permute-start | bytes 1597448 | tf_op jit(solution)/shard_map/ppermute | solution.py:22
  93.5 6.9 %collective-permute-start.35 = (bf16[520,512]{1,0:T(8,128)(2,1)S(1)}, bf16[520,512]{1,0:T(8,128)(2,1)S(1)}, u32[]{:S(2)}, u32[]{:S(2)}) collective-permute-start(bf16[520,512]{1,0:T(8,128)(2,1)S(1)} %get-tuple-element.41.refs_5_), channel_id=1, source_target_pairs={{0,4},{4,0},{8,12},{12,8},{16,20},{20,16},{24,28},{28,24},{1,5},{5... | collective-permute-start | bytes 1597448 | tf_op jit(solution)/shard_map/ppermute | solution.py:22
  94.4 7.4 %collective-permute-start.36 = (bf16[520,512]{1,0:T(8,128)(2,1)S(1)}, bf16[520,512]{1,0:T(8,128)(2,1)S(1)}, u32[]{:S(2)}, u32[]{:S(2)}) collective-permute-start(bf16[520,512]{1,0:T(8,128)(2,1)S(1)} %get-tuple-element.42.refs_6_), channel_id=1, source_target_pairs={{0,4},{4,0},{8,12},{12,8},{16,20},{20,16},{24,28},{28,24},{1,5},{5... | collective-permute-start | bytes 1597448 | tf_op jit(solution)/shard_map/ppermute | solution.py:22
  96.5 6.1 %collective-permute-start.14 = (bf16[520,512]{1,0:T(8,128)(2,1)S(1)}, bf16[520,512]{1,0:T(8,128)(2,1)S(1)}, u32[]{:S(2)}, u32[]{:S(2)}) collective-permute-start(bf16[520,512]{1,0:T(8,128)(2,1)S(1)} %collective-permute-done.12.refs_7_.refs_12_), channel_id=1, source_target_pairs={{0,4},{4,0},{8,12},{12,8},{16,20},{20,16},{24,28},{28,24},{1,5},{5... | collective-permute-start | bytes 1597448 | tf_op jit(solution)/shard_map/ppermute | solution.py:22
  104.9 15.1 %collective-permute-start.20 = (bf16[520,512]{1,0:T(8,128)(2,1)S(1)}, bf16[520,512]{1,0:T(8,128)(2,1)}, u32[]{:S(2)}, u32[]{:S(2)}) collective-permute-start(bf16[520,512]{1,0:T(8,128)(2,1)S(1)} %collective-permute-done.12.refs_7_.refs_12_), channel_id=1, source_target_pairs={{0,16},{4,20},{8,24},{12,28},{16,0},{20,4},{24,8},{28,12},{1,17},{... | collective-permute-start | bytes 1597448 | tf_op jit(solution)/shard_map/ppermute | solution.py:22
  106.9 15.1 %collective-permute-start.19 = (bf16[520,512]{1,0:T(8,128)(2,1)S(1)}, bf16[520,512]{1,0:T(8,128)(2,1)}, u32[]{:S(2)}, u32[]{:S(2)}) collective-permute-start(bf16[520,512]{1,0:T(8,128)(2,1)S(1)} %collective-permute-done.15.refs_10_.refs_19_), channel_id=1, source_target_pairs={{0,8},{4,12},{8,0},{12,4},{16,24},{20,28},{24,16},{28,20},{1,9},{5... | collective-permute-start | bytes 1597448 | tf_op jit(solution)/shard_map/ppermute | solution.py:22
  107.7 25.0 %collective-permute-start.30 = (bf16[520,512]{1,0:T(8,128)(2,1)}, bf16[520,512]{1,0:T(8,128)(2,1)}, u32[]{:S(2)}, u32[]{:S(2)}) collective-permute-start(bf16[520,512]{1,0:T(8,128)(2,1)} %collective-permute-done.29.refs_21_), channel_id=1, source_target_pairs={{0,8},{4,12},{8,0},{12,4},{16,24},{20,28},{24,16},{28,20},{1,9},{5... | collective-permute-start | bytes 1597448 | tf_op jit(solution)/shard_map/ppermute | solution.py:22
  109.0 23.7 %collective-permute-start.32 = (bf16[520,512]{1,0:T(8,128)(2,1)}, bf16[520,512]{1,0:T(8,128)(2,1)}, u32[]{:S(2)}, u32[]{:S(2)}) collective-permute-start(bf16[520,512]{1,0:T(8,128)(2,1)} %collective-permute-done.31.refs_14_), channel_id=1, source_target_pairs={{0,16},{4,20},{8,24},{12,28},{16,0},{20,4},{24,8},{28,12},{1,17},{... | collective-permute-start | bytes 1597448 | tf_op jit(solution)/shard_map/ppermute | solution.py:22
  109.2 24.1 %collective-permute-start.42 = (bf16[520,512]{1,0:T(8,128)(2,1)S(1)}, bf16[520,512]{1,0:T(8,128)(2,1)}, u32[]{:S(2)}, u32[]{:S(2)}) collective-permute-start(bf16[520,512]{1,0:T(8,128)(2,1)S(1)} %collective-permute-done.40.refs_22_), channel_id=1, source_target_pairs={{0,4},{4,0},{8,12},{12,8},{16,20},{20,16},{24,28},{28,24},{1,5},{5... | collective-permute-start | bytes 1597448 | tf_op jit(solution)/shard_map/ppermute | solution.py:22
  120.1 35.3 %collective-permute-start.22 = (bf16[520,512]{1,0:T(8,128)(2,1)}, bf16[520,512]{1,0:T(8,128)(2,1)S(1)}, u32[]{:S(2)}, u32[]{:S(2)}) collective-permute-start(bf16[520,512]{1,0:T(8,128)(2,1)} %collective-permute-done.20.refs_15_.refs_4_), channel_id=1, source_target_pairs={{0,4},{4,0},{8,12},{12,8},{16,20},{20,16},{24,28},{28,24},{1,5},{5... | collective-permute-start | bytes 1597448 | tf_op jit(solution)/shard_map/ppermute | solution.py:22
  122.0 33.3 %collective-permute-start.21 = (bf16[520,512]{1,0:T(8,128)(2,1)}, bf16[520,512]{1,0:T(8,128)(2,1)S(1)}, u32[]{:S(2)}, u32[]{:S(2)}) collective-permute-start(bf16[520,512]{1,0:T(8,128)(2,1)} %collective-permute-done.19.refs_14_.refs_3_), channel_id=1, source_target_pairs={{0,4},{4,0},{8,12},{12,8},{16,20},{20,16},{24,28},{28,24},{1,5},{5... | collective-permute-start | bytes 1597448 | tf_op jit(solution)/shard_map/ppermute | solution.py:22
  132.7 22.7 %collective-permute-start.33 = (bf16[520,512]{1,0:T(8,128)(2,1)}, bf16[520,512]{1,0:T(8,128)(2,1)S(1)}, u32[]{:S(2)}, u32[]{:S(2)}) collective-permute-start(bf16[520,512]{1,0:T(8,128)(2,1)} %collective-permute-done.30.refs_5_), channel_id=1, source_target_pairs={{0,4},{4,0},{8,12},{12,8},{16,20},{20,16},{24,28},{28,24},{1,5},{5... | collective-permute-start | bytes 1597448 | tf_op jit(solution)/shard_map/ppermute | solution.py:22
  132.7 22.7 %collective-permute-start.34 = (bf16[520,512]{1,0:T(8,128)(2,1)}, bf16[520,512]{1,0:T(8,128)(2,1)S(1)}, u32[]{:S(2)}, u32[]{:S(2)}) collective-permute-start(bf16[520,512]{1,0:T(8,128)(2,1)} %collective-permute-done.32.refs_6_), channel_id=1, source_target_pairs={{0,4},{4,0},{8,12},{12,8},{16,20},{20,16},{24,28},{28,24},{1,5},{5... | collective-permute-start | bytes 1597448 | tf_op jit(solution)/shard_map/ppermute | solution.py:22
  161.4 16.3 %collective-permute-start.45 = (bf16[384,512]{1,0:T(8,128)(2,1)S(1)}, bf16[384,512]{1,0:T(8,128)(2,1)S(1)}, u32[]{:S(2)}, u32[]{:S(2)}) collective-permute-start(bf16[384,512]{1,0:T(8,128)(2,1)S(1)} %get-tuple-element.49), channel_id=1, source_target_pairs={{0,1},{1,0},{2,3},{3,2},{4,5},{5,4},{6,7},{7,6},{8,9},{9,8},{10,11... | collective-permute-start | bytes 1179656 | tf_op jit(solution)/shard_map/ppermute | solution.py:22
  163.1 23.0 %collective-permute-start.43 = (bf16[384,512]{1,0:T(8,128)(2,1)S(1)}, bf16[384,512]{1,0:T(8,128)(2,1)S(1)}, u32[]{:S(2)}, u32[]{:S(2)}) collective-permute-start(bf16[384,512]{1,0:T(8,128)(2,1)S(1)} %get-tuple-element.46), channel_id=1, source_target_pairs={{0,1},{1,0},{2,3},{3,2},{4,5},{5,4},{6,7},{7,6},{8,9},{9,8},{10,11... | collective-permute-start | bytes 1179656 | tf_op jit(solution)/shard_map/ppermute | solution.py:22
  163.5 44.5 %collective-permute-start.47 = (bf16[384,256]{1,0:T(8,128)(2,1)S(1)}, bf16[384,256]{1,0:T(8,128)(2,1)S(1)}, u32[]{:S(2)}, u32[]{:S(2)}) collective-permute-start(bf16[384,256]{1,0:T(8,128)(2,1)S(1)} %get-tuple-element.52), channel_id=1, source_target_pairs={{0,1},{1,0},{2,3},{3,2},{4,5},{5,4},{6,7},{7,6},{8,9},{9,8},{10,11... | collective-permute-start | bytes 589832 | tf_op jit(solution)/shard_map/ppermute | solution.py:22
  165.1 44.2 %collective-permute-start.48 = (bf16[384,256]{1,0:T(8,128)(2,1)S(1)}, bf16[384,256]{1,0:T(8,128)(2,1)S(1)}, u32[]{:S(2)}, u32[]{:S(2)}) collective-permute-start(bf16[384,256]{1,0:T(8,128)(2,1)S(1)} %get-tuple-element.53), channel_id=1, source_target_pairs={{0,3},{1,2},{2,1},{3,0},{4,7},{5,6},{6,5},{7,4},{8,11},{9,10},{10,... | collective-permute-start | bytes 589832 | tf_op jit(solution)/shard_map/ppermute | solution.py:22
  167.5 41.7 %collective-permute-start.49 = (bf16[384,256]{1,0:T(8,128)(2,1)S(1)}, bf16[384,256]{1,0:T(8,128)(2,1)S(1)}, u32[]{:S(2)}, u32[]{:S(2)}) collective-permute-start(bf16[384,256]{1,0:T(8,128)(2,1)S(1)} %get-tuple-element.54), channel_id=1, source_target_pairs={{0,2},{1,3},{2,0},{3,1},{4,6},{5,7},{6,4},{7,5},{8,10},{9,11},{10,... | collective-permute-start | bytes 589832 | tf_op jit(solution)/shard_map/ppermute | solution.py:22
  177.6 28.5 %collective-permute-start.23 = (bf16[384,512]{1,0:T(8,128)(2,1)S(1)}, bf16[384,512]{1,0:T(8,128)(2,1)S(1)}, u32[]{:S(2)}, u32[]{:S(2)}) collective-permute-start(bf16[384,512]{1,0:T(8,128)(2,1)S(1)} %get-tuple-element.37), channel_id=1, source_target_pairs={{0,1},{1,0},{2,3},{3,2},{4,5},{5,4},{6,7},{7,6},{8,9},{9,8},{10,11... | collective-permute-start | bytes 1179656 | tf_op jit(solution)/shard_map/ppermute | solution.py:22
  186.1 23.2 %collective-permute-start.46 = (bf16[384,256]{1,0:T(8,128)(2,1)S(1)}, bf16[384,256]{1,0:T(8,128)(2,1)S(1)}, u32[]{:S(2)}, u32[]{:S(2)}) collective-permute-start(bf16[384,256]{1,0:T(8,128)(2,1)S(1)} %add_convert_fusion), channel_id=1, source_target_pairs={{0,2},{1,3},{2,0},{3,1},{4,6},{5,7},{6,4},{7,5},{8,10},{9,11},{10,... | collective-permute-start | bytes 589832 | tf_op jit(solution)/shard_map/ppermute | solution.py:22
  206.2 16.4 %collective-permute-start.44 = (bf16[384,256]{1,0:T(8,128)(2,1)S(1)}, bf16[384,256]{1,0:T(8,128)(2,1)S(1)}, u32[]{:S(2)}, u32[]{:S(2)}) collective-permute-start(bf16[384,256]{1,0:T(8,128)(2,1)S(1)} %add_convert_fusion.1), channel_id=1, source_target_pairs={{0,2},{1,3},{2,0},{3,1},{4,6},{5,7},{6,4},{7,5},{8,10},{9,11},{10,... | collective-permute-start | bytes 589832 | tf_op jit(solution)/shard_map/ppermute | solution.py:22
  208.0 17.7 %collective-permute-start.24 = (bf16[384,256]{1,0:T(8,128)(2,1)S(1)}, bf16[384,256]{1,0:T(8,128)(2,1)S(1)}, u32[]{:S(2)}, u32[]{:S(2)}) collective-permute-start(bf16[384,256]{1,0:T(8,128)(2,1)S(1)} %add_convert_fusion.2), channel_id=1, source_target_pairs={{0,2},{1,3},{2,0},{3,1},{4,6},{5,7},{6,4},{7,5},{8,10},{9,11},{10,... | collective-permute-start | bytes 589832 | tf_op jit(solution)/shard_map/ppermute | solution.py:22
  (40 other events, 290.4 us)
